TPU v7x, 32 devices: a whole 2x2x4 slice. The times are simulated.
32 devices in a mesh: row: 8 (over z, y), col: 4 (over x, core).
Axes of the slice: x: 2, y: 2, z: 4, core: 2. Of those that a mesh axis runs over, the one named last changes fastest.
Arguments:
- kernel_configs: float32 [4, 512, 2048], P(None, 'row', 'col'), may hold values from -1 to 2, as said below
- epoch_kernel: float32 [256, 256], replicated, may hold values from -1 to 2, as said below
- lengths: int32 [2048], P(('col', 'row')), may hold values from 1 to 256
- noise: float32 [2048], P(('col', 'row')), may hold values from 0.1 to 1
- curves: float32 [2048, 256], P(('col', 'row')), may hold values from -33 to 33
Outputs:
- solution: float32 [2048, 256], P(('col', 'row'))
- residual: float32 [2048, 256], P(('col', 'row'))
Inputs may be any that keep to these rules, and one draw needn't show every extreme that they name: `kernel_configs`: reshaped to 2048 x 2048 by merging the first two dimensions, the matrix is symmetric positive definite. `epoch_kernel`: symmetric positive definite.
All inputs are finite; a program needn't handle non-finite values.
Results may differ from a plain program's by a relative error of at most 0.00026.
Values sent between devices are 32-bit elements; how exact they have to be, the bound alone decides.
A program may use at most 64 MiB of HBM per device.

v0:
```python
import jax
import jax.numpy as jnp
from jax import lax
from jax.sharding import PartitionSpec as P

ITERS = 2


def per_device(kernel_configs, epoch_kernel, lengths, noise, curves):
    row_count = curves.shape[0]
    epochs = curves.shape[1]
    epoch_index = lax.broadcasted_iota(jnp.int32, (row_count, epochs), 1)
    curve_mask = (epoch_index < lengths[:, None]).astype(jnp.float32)
    local_tile = kernel_configs.reshape(-1, kernel_configs.shape[2])

    def operate(vector):
        masked = vector * curve_mask
        partial_value = jnp.dot(
            local_tile,
            lax.all_gather(masked, "row", axis=0, tiled=True),
            precision=lax.Precision.HIGHEST,
            preferred_element_type=jnp.float32,
        )
        summed = lax.psum_scatter(partial_value, "col", scatter_dimension=0, tiled=True)
        smoothed = jnp.dot(
            summed,
            epoch_kernel,
            precision=lax.Precision.HIGHEST,
            preferred_element_type=jnp.float32,
        )
        return curve_mask * smoothed + noise[:, None] * vector

    def two_products(residual, applied):
        return lax.psum((jnp.sum(residual * residual), jnp.sum(residual * applied)), ("row", "col"))

    solution = jnp.zeros_like(curves)
    residual = curves * curve_mask
    applied = operate(residual)
    norm_now, curvature_sum = two_products(residual, applied)
    step_size = norm_now / curvature_sum
    direction = residual
    direction_image = applied
    for iteration in range(ITERS):
        solution = solution + step_size * direction
        residual = residual - step_size * direction_image
        if iteration + 1 < ITERS:
            applied = operate(residual)
            norm_next, curvature_sum = two_products(residual, applied)
            beta_ratio = norm_next / norm_now
            step_size = norm_next / (curvature_sum - beta_ratio * norm_next / step_size)
            direction = residual + beta_ratio * direction
            direction_image = applied + beta_ratio * direction_image
            norm_now = norm_next
    return (solution, residual)


def solution(mesh):
    in_specs = (
        P(None, "row", "col"),
        P(),
        P(("col", "row")),
        P(("col", "row")),
        P(("col", "row"), None),
    )
    out_specs = (P(("col", "row"), None), P(("col", "row"), None))
    return jax.shard_map(
        per_device, mesh=mesh, in_specs=in_specs, out_specs=out_specs, check_vma=False
    )
```

profile of v0, /device:TPU:0, one launch (start us, length us, event | category | flops | bytes accessed | tf_op | source)
XLA Modules:
  0.0 215.1 jit_solution(16533461763690176692)
XLA Ops:
  7.2 0.0 copy-start
  7.2 0.0 reduce-scatter.7.cloned.1.call-start
  7.2 1.0 fusion.3
  8.2 33.0 %all_gather.6 = f32[512,256]{1,0:T(8,128)S(1)} all-gather(f32[64,256]{1,0:T(8,128)S(1)} %fusion.3), channel_id=1, replica_groups=mesh['row'=8,'col'=4] {'row'}, dimensions={0}, use_global_device_ids=true | all-gather | bytes 589824 | tf_op jit(solution)/shard_map/all_gather | solution.py:20
  41.2 0.0 copy-done
  41.2 1.0 convolution_bitcast_fusion.1
  42.3 0.0 copy-start.2
  42.3 0.8 copy.7
  43.1 0.0 copy-start.1
  43.1 0.0 copy-start.3
  43.1 0.0 copy-start.4
  43.1 0.0 reduce-scatter.7.cloned.1.call-update
  43.1 0.0 reduce-scatter.9.cloned.1.call-start
  43.2 21.3 %reduce-scatter.7.cloned.1.call-done = f32[64,256]{1,0:T(8,128)} async-done(((f32[256,256]{1,0:T(8,128)}), f32[64,256]{1,0:T(8,128)}) %reduce-scatter.7.cloned.1.call-update) | async-done | bytes 65552
  64.5 0.0 copy-done.2
  64.5 0.0 copy-done.1
  64.5 0.0 copy-done.3
  64.5 0.0 copy-done.4
  64.5 1.7 multiply_reduce_fusion.2
  66.2 39.6 %all-reduce.1 = (f32[]{:T(128)}, f32[]{:T(128)}) all-reduce(f32[]{:T(128)} %get-tuple-element.3, f32[]{:T(128)} %get-tuple-element.2), channel_id=1, replica_groups=mesh['row'=8,'col'=4] {'row','col'}, use_global_device_ids=true, to_apply=%region_1.0 | all-reduce | flops 2 | bytes 16 | tf_op jit(solution)/shard_map/psum | solution.py:34
  107.1 0.1 fusion.2
  107.2 31.3 %all_gather.7 = f32[512,256]{1,0:T(8,128)S(1)} all-gather(f32[64,256]{1,0:T(8,128)S(1)} %get-tuple-element.10), channel_id=1, replica_groups=mesh['row'=8,'col'=4] {'row'}, dimensions={0}, use_global_device_ids=true | all-gather | bytes 589824 | tf_op jit(solution)/shard_map/all_gather | solution.py:20
  138.5 1.0 convolution_bitcast_fusion
  139.5 0.8 copy.9
  140.3 0.0 reduce-scatter.9.cloned.1.call-update
  140.3 21.3 %reduce-scatter.9.cloned.1.call-done = f32[64,256]{1,0:T(8,128)} async-done(((f32[256,256]{1,0:T(8,128)}), f32[64,256]{1,0:T(8,128)}) %reduce-scatter.9.cloned.1.call-update) | async-done | bytes 65552
  161.6 1.8 multiply_reduce_fusion
  163.4 39.6 %all-reduce = (f32[]{:T(128)}, f32[]{:T(128)}) all-reduce(f32[]{:T(128)} %get-tuple-element.5, f32[]{:T(128)} %get-tuple-element.4), channel_id=1, replica_groups=mesh['row'=8,'col'=4] {'row','col'}, use_global_device_ids=true, to_apply=%region_6.0 | all-reduce | flops 2 | bytes 16 | tf_op jit(solution)/shard_map/psum | solution.py:34
  207.5 0.7 multiply_subtract_fusion
Async XLA Ops:
  7.2 34.1 %copy-start = (f32[4,64,512]{2,1,0:T(8,128)S(1)}, f32[4,64,512]{2,1,0:T(8,128)}, u32[]{:S(2)}) copy-start(f32[4,64,512]{2,1,0:T(8,128)} %param.5) | copy-start | bytes 1572868
  7.2 57.3 %reduce-scatter.7.cloned.1.call-start = ((), (), s32[]{:S(2)}) async-start(), calls=%async_computation.2 | async-start | bytes 327680
  42.3 22.2 %copy-start.2 = (f32[64,256]{1,0:T(8,128)S(1)}, f32[64,256]{1,0:T(8,128)}, u32[]{:S(2)}) copy-start(f32[64,256]{1,0:T(8,128)} %param.9) | copy-start | bytes 196612
  43.1 21.3 %copy-start.1 = (f32[256,256]{1,0:T(8,128)S(1)}, f32[256,256]{1,0:T(8,128)}, u32[]{:S(2)}) copy-start(f32[256,256]{1,0:T(8,128)} %param.6) | copy-start | bytes 786436
  43.1 21.3 %copy-start.3 = (s32[64]{0:T(128)S(1)}, s32[64]{0:T(128)}, u32[]{:S(2)}) copy-start(s32[64]{0:T(128)} %param.7) | copy-start | bytes 772
  43.1 21.3 %copy-start.4 = (f32[64]{0:T(128)S(1)}, f32[64]{0:T(128)}, u32[]{:S(2)}) copy-start(f32[64]{0:T(128)} %param.8) | copy-start | bytes 772
  43.1 118.5 %reduce-scatter.9.cloned.1.call-start = ((), (), s32[]{:S(2)}) async-start(), calls=%async_computation.3 | async-start | bytes 327680
Sparse Core Ops, SparseCore 0:
  43.3 21.1 reduce-scatter.6
  140.5 21.1 reduce-scatter.8
where the time goes:
time: 216 us; the launch traced here: 215 us
  blocking collectives  143 us (66%)
  waiting for transfers between devices  42.6 us (20%)
  between operations  20 us (9%)
  matrix products  5.53 us (3%)
    psum x2, blocking collectives, two_products(): lax.psum((jnp.sum(residual * residual), jnp.sum(residual * applied)), ('r...  79.1 us
    all_gather x2, blocking collectives, operate(): lax.all_gather(masked, 'row', axis=0, tiled=True)  64.3 us
    unnamed x4, waiting for transfers between devices  42.6 us
  transfers between devices with their start and end apart: 2, of which 2 were waited for; matrix products, arithmetic and copies ran while one was open for 0% of the time, Pallas kernels for 0%

commit v1 on v0

v1 whole, which is shorter than its diff:
```python
import functools

import jax
import jax.numpy as jnp
from jax import lax
from jax.experimental import pallas as pl
from jax.experimental.pallas import tpu as pltpu
from jax.sharding import PartitionSpec as P

MESH = pl.DeviceIdType.MESH
HALVES = 2
INNER = 2


def flip(index, bits):
    place = 1
    result = index
    while place <= bits:
        if (bits // place) % 2:
            result = result + place * (1 - 2 * ((index // place) % 2))
        place *= 2
    return result


def split(value):
    high = value.astype(jnp.bfloat16)
    low = (value - high.astype(jnp.float32)).astype(jnp.bfloat16)
    return high, low


def dot3(left, right):
    mul = functools.partial(jnp.dot, preferred_element_type=jnp.float32)
    return mul(left[0], right[0]) + (mul(left[0], right[1]) + mul(left[1], right[0]))


def fold(value):
    rows, epochs = value.shape
    tiles = [
        value[i : i + 8, j : j + 128] for i in range(0, rows, 8) for j in range(0, epochs, 128)
    ]
    while len(tiles) > 1:
        tiles = [sum(tiles[i : i + 2][1:], tiles[i]) for i in range(0, len(tiles), 2)]
    return tiles[0]


def total(tile):
    return jnp.sum(jnp.sum(tile, axis=0, keepdims=True), axis=1, keepdims=True)


def column(row):
    n = row.shape[1]
    one = lax.broadcasted_iota(jnp.int32, (n, n), 0)
    two = lax.broadcasted_iota(jnp.int32, (n, n), 1)
    return jnp.sum(jnp.where(one == two, row, jnp.zeros_like(row)), axis=1, keepdims=True)


def kernel(
    R, C,
    tile_hbm, epoch_hbm, lengths_hbm, noise_hbm, curves_hbm,
    solution_ref, residual_ref,
    tile, epoch, lengths, noise, curves,
    tile_high, tile_low, epoch_high, epoch_low,
    gathered, partial, arrived, sums_col, sums_row,
    load_sem, line_send, line_recv, pair_send, pair_recv,
    part_send, part_recv, col_send, col_recv, row_send, row_recv,
):
    L = R // INNER
    me_row = lax.axis_index("row")
    me_col = lax.axis_index("col")
    outer = me_row // INNER
    inner = me_row % INNER
    other = 1 - inner
    rows, epochs = curves.shape
    width = epochs // HALVES

    loads = []
    for i, (src, dst) in enumerate(
        ((curves_hbm, curves), (lengths_hbm, lengths), (noise_hbm, noise),
         (tile_hbm, tile), (epoch_hbm, epoch))
    ):
        load = pltpu.make_async_copy(src, dst, load_sem.at[i])
        load.start()
        loads.append(load)

    barrier = pltpu.get_barrier_semaphore()
    for k in range(1, R):
        pl.semaphore_signal(barrier, inc=1, device_id=(flip(me_row, k), me_col), device_id_type=MESH)
    for j in range(1, C):
        pl.semaphore_signal(barrier, inc=1, device_id=(me_row, flip(me_col, j)), device_id_type=MESH)

    for load in loads[:3]:
        load.wait()
    length_col = column(lengths[...].astype(jnp.float32))
    noise_col = column(noise[...])
    position = lax.broadcasted_iota(jnp.int32, (rows, epochs), 1).astype(jnp.float32)
    mask = position < length_col
    first = jnp.where(mask, curves[...], 0.0)

    def remote(src, dst, send, recv, target):
        copy = pltpu.make_async_remote_copy(
            src_ref=src, dst_ref=dst, send_sem=send, recv_sem=recv,
            device_id=target, device_id_type=MESH,
        )
        return copy

    def place(op, h, k, side):
        return gathered.at[op, h, flip(outer, k) * INNER + side]

    def line_copy(op, h, k):
        return remote(
            place(op, h, 0, inner), place(op, h, 0, inner),
            line_send.at[op, h, k], line_recv.at[op, h, k],
            (flip(outer, k) * INNER + inner, me_col),
        )

    def line_arrival(op, h, k):
        return remote(
            place(op, h, k, inner), place(op, h, k, inner),
            line_send.at[op, h, k], line_recv.at[op, h, k],
            (flip(outer, k) * INNER + inner, me_col),
        )

    def pair_copy(op, h, k):
        return remote(
            place(op, h, k, inner), place(op, h, k, inner),
            pair_send.at[op, h, k], pair_recv.at[op, h, k],
            (outer * INNER + other, me_col),
        )

    def pair_arrival(op, h, k):
        return remote(
            place(op, h, k, other), place(op, h, k, other),
            pair_send.at[op, h, k], pair_recv.at[op, h, k],
            (outer * INNER + other, me_col),
        )

    def part_copy(op, h, j):
        return remote(
            partial.at[op, h, flip(me_col, j)], arrived.at[op, h, j - 1],
            part_send.at[op, h, j], part_recv.at[op, h, j],
            (me_row, flip(me_col, j)),
        )

    def col_copy(t, j):
        return remote(
            sums_col.at[t, 0], sums_col.at[t, j],
            col_send.at[t, j], col_recv.at[t, j],
            (me_row, flip(me_col, j)),
        )

    def row_copy(t, k):
        return remote(
            sums_row.at[t, 0], sums_row.at[t, k],
            row_send.at[t, k], row_recv.at[t, k],
            (flip(me_row, k), me_col),
        )

    def spread(op, field):
        for h in range(HALVES):
            gathered[op, h, me_row] = field[:, h * width : (h + 1) * width]
            for k in range(1, L):
                line_copy(op, h, k).start()
            pair_copy(op, h, 0).start()

    def relay(op):
        for h in range(HALVES):
            for k in range(1, L):
                line_arrival(op, h, k).wait_recv()
                pair_copy(op, h, k).start()

    def multiply(op):
        for h in range(HALVES):
            for k in range(L):
                pair_arrival(op, h, k).wait_recv()
            block = split(gathered[op, h].reshape(R * rows, width))
            product = dot3((tile_high[...], tile_low[...]), block)
            partial[op, h] = product.reshape(C, rows, width)
            for j in range(1, C):
                part_copy(op, h, j).start()

    def finish(op, field):
        smoothed = None
        for h in range(HALVES):
            value = partial[op, h, me_col]
            for j in range(1, C):
                part_copy(op, h, j).wait_recv()
                value = value + arrived[op, h, j - 1]
            cut = slice(h * width, (h + 1) * width)
            term = dot3(split(value), (epoch_high[cut, :], epoch_low[cut, :]))
            smoothed = term if smoothed is None else smoothed + term
        return jnp.where(mask, smoothed, 0.0) + noise_col * field

    def drain(op):
        for h in range(HALVES):
            for k in range(1, L):
                line_copy(op, h, k).wait_send()
            for k in range(L):
                pair_copy(op, h, k).wait_send()
            for j in range(1, C):
                part_copy(op, h, j).wait_send()

    def sums_start(t, one, two):
        sums_col[t, 0, 0] = fold(one)
        sums_col[t, 0, 1] = fold(two)
        for j in range(1, C):
            col_copy(t, j).start()

    def sums_pass(t):
        for j in range(1, C):
            col_copy(t, j).wait_recv()
        value = sums_col[t, 0]
        for j in range(1, C):
            value = value + sums_col[t, j]
        sums_row[t, 0] = value
        for k in range(1, R):
            row_copy(t, k).start()

    def sums_end(t):
        for k in range(1, R):
            row_copy(t, k).wait_recv()
        value = sums_row[t, 0]
        for k in range(1, R):
            value = value + sums_row[t, k]
        return total(value[0]), total(value[1])

    def sums_drain(t):
        for j in range(1, C):
            col_copy(t, j).wait_send()
        for k in range(1, R):
            row_copy(t, k).wait_send()

    pl.semaphore_wait(barrier, R - 1 + C - 1)
    spread(0, first)
    for load in loads[3:]:
        load.wait()
    high, low = split(tile[...].reshape(C * rows, R * rows))
    tile_high[...] = high
    tile_low[...] = low
    high, low = split(epoch[...])
    epoch_high[...] = high
    epoch_low[...] = low
    relay(0)
    multiply(0)
    image = finish(0, first)

    spread(1, image)
    sums_start(0, first * first, first * image)
    sums_pass(0)
    relay(1)
    norm_first, curvature = sums_end(0)
    step = norm_first / curvature
    second = first - step * image
    multiply(1)
    image_second = image - step * finish(1, image)

    sums_start(1, second * second, second * image_second)
    sums_pass(1)
    drain(0)
    drain(1)
    norm_second, curvature = sums_end(1)
    ratio = norm_second / norm_first
    step_second = norm_second / (curvature - ratio * norm_second / step)
    solution_ref[...] = step * first + step_second * (second + ratio * first)
    residual_ref[...] = second - step_second * (image_second + ratio * image)
    sums_drain(0)
    sums_drain(1)


def per_device(R, C, kernel_configs, epoch_kernel, lengths, noise, curves):
    rows, epochs = curves.shape
    L = R // INNER
    width = epochs // HALVES
    f32 = jnp.float32
    bf16 = jnp.bfloat16
    dma = pltpu.SemaphoreType.DMA
    return pl.pallas_call(
        functools.partial(kernel, R, C),
        out_shape=[jax.ShapeDtypeStruct((rows, epochs), f32)] * 2,
        in_specs=[pl.BlockSpec(memory_space=pl.ANY)] * 5,
        out_specs=[pl.BlockSpec(memory_space=pltpu.VMEM)] * 2,
        scratch_shapes=[
            pltpu.VMEM(kernel_configs.shape, f32),
            pltpu.VMEM((epochs, epochs), f32),
            pltpu.VMEM((1, rows), jnp.int32),
            pltpu.VMEM((1, rows), f32),
            pltpu.VMEM((rows, epochs), f32),
            pltpu.VMEM((C * rows, R * rows), bf16),
            pltpu.VMEM((C * rows, R * rows), bf16),
            pltpu.VMEM((epochs, epochs), bf16),
            pltpu.VMEM((epochs, epochs), bf16),
            pltpu.VMEM((2, HALVES, R, rows, width), f32),
            pltpu.VMEM((2, HALVES, C, rows, width), f32),
            pltpu.VMEM((2, HALVES, C - 1, rows, width), f32),
            pltpu.VMEM((2, C, 2, 8, 128), f32),
            pltpu.VMEM((2, R, 2, 8, 128), f32),
            dma((5,)),
            dma((2, HALVES, L)),
            dma((2, HALVES, L)),
            dma((2, HALVES, L)),
            dma((2, HALVES, L)),
            dma((2, HALVES, C)),
            dma((2, HALVES, C)),
            dma((2, C)),
            dma((2, C)),
            dma((2, R)),
            dma((2, R)),
        ],
        compiler_params=pltpu.CompilerParams(collective_id=0, has_side_effects=True),
        name="cg",
    )(kernel_configs, epoch_kernel, lengths.reshape(1, -1), noise.reshape(1, -1), curves)


def solution(mesh):
    in_specs = (
        P(None, "row", "col"),
        P(),
        P(("col", "row")),
        P(("col", "row")),
        P(("col", "row"), None),
    )
    out_specs = (P(("col", "row"), None), P(("col", "row"), None))
    body = functools.partial(per_device, mesh.shape["row"], mesh.shape["col"])
    return jax.shard_map(body, mesh=mesh, in_specs=in_specs, out_specs=out_specs, check_vma=False)
```

time: 216 us -> 46.4 us (0.21)
  blocking collectives: 143 us -> 0 us
  Pallas kernels: 0 us -> 43.4 us
  waiting for transfers between devices: 42.6 us -> 0 us
  between operations: 20 us -> 0.65 us
  matrix products: 5.53 us -> 0 us
    psum x2 -> x0, blocking collectives: 79.1 us -> none  [two_products(): lax.psum((jnp.sum(residual * residual), jnp.sum(residual * applied)), ('r...]
    all_gather x2 -> x0, blocking collectives: 64.3 us -> none  [operate(): lax.all_gather(masked, 'row', axis=0, tiled=True)]
    pallas_call x0 -> x1, Pallas kernels: none -> 43.4 us  [per_device(): pl.pallas_call(functools.partial(kernel, R, C), out_shape=[jax.ShapeDtype...]
    unnamed x4 -> x0, waiting for transfers between devices: 42.6 us -> none
    dot_general x4 -> x0, matrix products: 5.53 us -> none  [the longest x2 3.49 us: operate(): jnp.dot(summed, epoch_kernel, precision=lax.Precision.HIGHEST, preferred_...]
  transfers between devices with their start and end apart: 2 -> 0, of which waited for: 2 -> 0; matrix products, arithmetic and copies ran while one was open for 0% -> 0% of each run, Pallas kernels for 0% -> 0%
where the time goes in v1:
time: 46.4 us; the launch traced here: 46.2 us
  Pallas kernels  43.4 us (94%)
  local copies, waits for them, and re-layouts  2.14 us (5%)
  between operations  0.65 us (1%)
    pallas_call x1, Pallas kernels, per_device(): pl.pallas_call(functools.partial(kernel, R, C), out_shape=[jax.ShapeDtype...  43.4 us
    unnamed x4, local copies, waits for them, and re-layouts  2.14 us

profile of v1, /device:TPU:0, one launch (start us, length us, event | category | flops | bytes accessed | tf_op | source)
XLA Modules:
  0.0 46.2 jit_solution(1333679130565984525)
XLA Ops:
  0.6 43.4 %cg.1 = (f32[64,256]{1,0:T(8,128)}, f32[64,256]{1,0:T(8,128)}) custom-call(f32[4,64,512]{2,1,0:T(8,128)} %tile_hbm.1, f32[256,256]{1,0:T(8,128)} %epoch_hbm.1, s32[1,64]{1,0:T(1,128)} %bitcast.2, f32[1,64]{1,0:T(1,128)} %bitcast.3, f32[64,256]{1,0:T(8,128)} %curves_hbm.1), custom_call_target="tpu_custom_call" | custom-call | tf_op jit(solution)/shard_map/cg/pallas_call | solution.py:276
  44.1 0.0 copy-start
  44.1 1.5 %copy.9 = f32[64,256]{1,0:T(8,128)} copy(f32[64,256]{1,0:T(8,128)} %get-tuple-element.4) | data formatting | bytes 131072
  45.6 0.0 copy-done
  45.6 0.6 %copy.10 = f32[64,256]{1,0:T(8,128)} copy(f32[64,256]{1,0:T(8,128)S(1)} %copy-done) | data formatting | bytes 131072
Async XLA Ops:
  44.1 1.5 %copy-start = (f32[64,256]{1,0:T(8,128)S(1)}, f32[64,256]{1,0:T(8,128)}, u32[]{:S(2)}) copy-start(f32[64,256]{1,0:T(8,128)} %get-tuple-element.5) | copy-start | bytes 196612

commit v2 on v1

v2 whole, which is shorter than its diff:
```python
import functools
import math

import jax
import jax.numpy as jnp
from jax import lax
from jax.experimental import pallas as pl
from jax.experimental.pallas import tpu as pltpu
from jax.sharding import PartitionSpec as P

MESH = pl.DeviceIdType.MESH
HALVES = 2
GROUP = 2


def flip(index, bits):
    place = 1
    result = index
    while place <= bits:
        if (bits // place) % 2:
            result = result + place * (1 - 2 * ((index // place) % 2))
        place *= 2
    return result


def split(value):
    high = value.astype(jnp.bfloat16)
    low = (value - high.astype(jnp.float32)).astype(jnp.bfloat16)
    return high, low


def dot3(left, right):
    mul = functools.partial(jnp.dot, preferred_element_type=jnp.float32)
    return mul(left[0], right[0]) + (mul(left[0], right[1]) + mul(left[1], right[0]))


def fold(value):
    rows, epochs = value.shape
    tiles = [
        value[i : i + 8, j : j + 128] for i in range(0, rows, 8) for j in range(0, epochs, 128)
    ]
    while len(tiles) > 1:
        tiles = [sum(tiles[i : i + 2][1:], tiles[i]) for i in range(0, len(tiles), 2)]
    return tiles[0]


def column(row):
    n = row.shape[1]
    one = lax.broadcasted_iota(jnp.int32, (n, n), 0)
    two = lax.broadcasted_iota(jnp.int32, (n, n), 1)
    return jnp.sum(jnp.where(one == two, row, jnp.zeros_like(row)), axis=1, keepdims=True)


def kernel(
    R, C,
    tile_hbm, epoch_hbm, lengths_hbm, noise_hbm, curves_hbm,
    solution_ref, residual_ref,
    tile, epoch, lengths, noise, curves,
    tile_high, tile_low, epoch_high, epoch_low,
    gathered, crossed, partial, arrived, sums,
    load_sem, row_send, row_recv,
    cross_send, cross_recv, part_send, part_recv, sums_send, sums_recv,
):
    N = R * C
    me_row = lax.axis_index("row")
    me_col = lax.axis_index("col")
    rows, epochs = curves.shape
    width = epochs // HALVES

    loads = []
    for i, (src, dst) in enumerate(
        ((curves_hbm, curves), (lengths_hbm, lengths), (noise_hbm, noise),
         (tile_hbm, tile), (epoch_hbm, epoch))
    ):
        load = pltpu.make_async_copy(src, dst, load_sem.at[i])
        load.start()
        loads.append(load)

    def row_target(d):
        return (flip(me_row, d), me_col)

    def col_target(j):
        return (me_row, flip(me_col, j))

    barrier = pltpu.get_barrier_semaphore()

    def greet(target):
        pl.semaphore_signal(barrier, inc=1, device_id=target, device_id_type=MESH)

    direct = [*range(GROUP, R, GROUP), *range(1, GROUP)]
    for d in direct:
        greet(row_target(d))
    for j in range(1, C):
        greet(col_target(j))

    for load in loads[:3]:
        load.wait()
    length_col = column(lengths[...].astype(jnp.float32))
    noise_col = column(noise[...])
    position = lax.broadcasted_iota(jnp.int32, (rows, epochs), 1).astype(jnp.float32)
    mask = position < length_col
    first = jnp.where(mask, curves[...], 0.0)

    def remote(src, dst, send, recv, target):
        return pltpu.make_async_remote_copy(
            src_ref=src, dst_ref=dst, send_sem=send, recv_sem=recv,
            device_id=target, device_id_type=MESH,
        )

    def row_copy(op, h, d):
        near = d % GROUP
        far = d - near
        held, step = (far, near) if far and near else (0, d)
        block = gathered.at[op, h, flip(me_row, held)]
        return remote(block, block, row_send.at[op, h, d], row_recv.at[op, h, d], row_target(step))

    def row_arrival(op, h, d):
        block = gathered.at[op, h, flip(me_row, d)]
        return remote(block, block, row_send.at[op, h, d], row_recv.at[op, h, d], row_target(1))

    def cross_copy(op, j, at):
        block = crossed.at[op, at]
        return remote(block, block, cross_send.at[op, j], cross_recv.at[op, j], col_target(j))

    def part_copy(op, h, j):
        return remote(
            partial.at[op, h, flip(me_col, j)], arrived.at[op, h, j - 1],
            part_send.at[op, h, j], part_recv.at[op, h, j], col_target(j),
        )

    def spread(op, field):
        for h in range(HALVES):
            gathered[op, h, me_row] = field[:, h * width : (h + 1) * width]
            for d in direct:
                row_copy(op, h, d).start()
        crossed[op, me_col] = field
        for j in range(1, C):
            cross_copy(op, j, me_col).start()

    def relay(op):
        for h in range(HALVES):
            for far in range(GROUP, R, GROUP):
                row_arrival(op, h, far).wait_recv()
                for near in range(1, GROUP):
                    row_copy(op, h, far + near).start()

    def multiply(op):
        for h in range(HALVES):
            for d in range(1, R):
                if d < GROUP or d % GROUP:
                    row_arrival(op, h, d).wait_recv()
            block = split(gathered[op, h].reshape(R * rows, width))
            product = dot3((tile_high[...], tile_low[...]), block)
            partial[op, h] = product.reshape(C, rows, width)
            for j in range(1, C):
                part_copy(op, h, j).start()

    def finish(op, field):
        smoothed = None
        for h in range(HALVES):
            value = partial[op, h, me_col]
            for j in range(1, C):
                part_copy(op, h, j).wait_recv()
                value = value + arrived[op, h, j - 1]
            cut = slice(h * width, (h + 1) * width)
            term = dot3(split(value), (epoch_high[cut, :], epoch_low[cut, :]))
            smoothed = term if smoothed is None else smoothed + term
        return jnp.where(mask, smoothed, 0.0) + noise_col * field

    def drain(op):
        for h in range(HALVES):
            for d in range(1, R):
                row_copy(op, h, d).wait_send()
            for j in range(1, C):
                part_copy(op, h, j).wait_send()
        for j in range(1, C):
            cross_copy(op, j, me_col).wait_send()

    def sums_start(t, one, two):
        sums[t, 0, :, :128] = jnp.sum(one, axis=0, keepdims=True)
        sums[t, 0, :, 128:] = jnp.sum(two, axis=0, keepdims=True)
        for d in range(1, N):
            remote(
                sums.at[t, 0], sums.at[t, d], sums_send.at[t], sums_recv.at[t],
                (flip(me_row, d // C), flip(me_col, d % C)),
            ).start()

    def sums_all(t):
        block = sums.at[t, pl.ds(1, N - 1)]
        return remote(block, block, sums_send.at[t], sums_recv.at[t], row_target(1))

    def sums_end(t):
        sums_all(t).wait_recv()
        value = sums[t, 0]
        for d in range(1, N):
            value = value + sums[t, d]
        return (
            jnp.sum(value[:, :128], axis=1, keepdims=True),
            jnp.sum(value[:, 128:], axis=1, keepdims=True),
        )

    pl.semaphore_wait(barrier, len(direct) + C - 1)
    spread(0, first)
    for load in loads[3:]:
        load.wait()
    high, low = split(tile[...].reshape(C * rows, R * rows))
    tile_high[...] = high
    tile_low[...] = low
    high, low = split(epoch[...])
    epoch_high[...] = high
    epoch_low[...] = low
    relay(0)
    multiply(0)
    image = finish(0, first)

    spread(1, image)
    sums_start(0, fold(first * first), fold(first * image))
    relay(1)
    norm_first, curvature = sums_end(0)
    step = norm_first / curvature
    second = first - step * image
    norm_tile = fold(second * second)
    noise_tile = fold(noise_col * second * second)
    for op in range(2):
        for j in range(1, C):
            cross_copy(op, j, flip(me_col, j)).wait_recv()
    weight = (crossed[0] - step * crossed[1]).reshape(C * rows, epochs)
    weight = dot3(split(weight), (epoch_high[...], epoch_low[...]))
    multiply(1)
    for h in range(HALVES):
        difference = (partial[0, h] - step * partial[1, h]).reshape(C * rows, width)
        noise_tile = noise_tile + fold(weight[:, h * width : (h + 1) * width] * difference)
    sums_start(1, norm_tile, noise_tile)
    image_second = image - step * finish(1, image)
    drain(0)
    drain(1)
    norm_second, curvature = sums_end(1)
    ratio = norm_second / norm_first
    step_second = norm_second / (curvature - ratio * norm_second / step)
    solution_ref[...] = step * first + step_second * (second + ratio * first)
    residual_ref[...] = second - step_second * (image_second + ratio * image)
    for t in range(2):
        sums_all(t).wait_send()


def per_device(R, C, kernel_configs, epoch_kernel, lengths, noise, curves):
    rows, epochs = curves.shape
    width = epochs // HALVES
    f32 = jnp.float32
    bf16 = jnp.bfloat16
    dma = pltpu.SemaphoreType.DMA
    buffers = [
        (kernel_configs.shape, f32),
        ((epochs, epochs), f32),
        ((1, rows), jnp.int32),
        ((1, rows), f32),
        ((rows, epochs), f32),
        ((C * rows, R * rows), bf16),
        ((C * rows, R * rows), bf16),
        ((epochs, epochs), bf16),
        ((epochs, epochs), bf16),
        ((2, HALVES, R, rows, width), f32),
        ((2, C, rows, epochs), f32),
        ((2, HALVES, C, rows, width), f32),
        ((2, HALVES, C - 1, rows, width), f32),
        ((2, R * C, 1, 256), f32),
    ]
    held = sum(math.prod(shape) * jnp.dtype(kind).itemsize for shape, kind in buffers)
    return pl.pallas_call(
        functools.partial(kernel, R, C),
        out_shape=[jax.ShapeDtypeStruct((rows, epochs), f32)] * 2,
        in_specs=[pl.BlockSpec(memory_space=pltpu.HBM)] * 5,
        out_specs=[pl.BlockSpec(memory_space=pltpu.VMEM)] * 2,
        scratch_shapes=[pltpu.VMEM(shape, kind) for shape, kind in buffers]
        + [
            dma((5,)),
            dma((2, HALVES, R)),
            dma((2, HALVES, R)),
            dma((2, C)),
            dma((2, C)),
            dma((2, HALVES, C)),
            dma((2, HALVES, C)),
            dma((2,)),
            dma((2,)),
        ],
        compiler_params=pltpu.CompilerParams(
            collective_id=0, has_side_effects=True,

        ),
        name="cg",
    )(kernel_configs, epoch_kernel, lengths.reshape(1, -1), noise.reshape(1, -1), curves)


def solution(mesh):
    in_specs = (
        P(None, "row", "col"),
        P(),
        P(("col", "row")),
        P(("col", "row")),
        P(("col", "row"), None),
    )
    out_specs = (P(("col", "row"), None), P(("col", "row"), None))
    body = functools.partial(per_device, mesh.shape["row"], mesh.shape["col"])
    return jax.shard_map(body, mesh=mesh, in_specs=in_specs, out_specs=out_specs, check_vma=False)
```

time: 46.4 us -> 40 us (0.86)
  Pallas kernels: 43.4 us -> 37 us
    pallas_call x1, Pallas kernels: 43.4 us -> 37 us  [per_device(): pl.pallas_call(functools.partial(kernel, R, C), out_shape=[jax.ShapeDtype...]
where the time goes in v2:
time: 40 us; the launch traced here: 39.8 us
  Pallas kernels  37 us (92%)
  local copies, waits for them, and re-layouts  2.14 us (5%)
  between operations  0.65 us (2%)
    pallas_call x1, Pallas kernels, per_device(): pl.pallas_call(functools.partial(kernel, R, C), out_shape=[jax.ShapeDtype...  37 us
    unnamed x4, local copies, waits for them, and re-layouts  2.14 us

profile of v2, /device:TPU:0, one launch (start us, length us, event | category | flops | bytes accessed | tf_op | source)
XLA Modules:
  0.0 39.8 jit_solution(15226177476390571064)
XLA Ops:
  0.6 37.0 %cg.1 = (f32[64,256]{1,0:T(8,128)}, f32[64,256]{1,0:T(8,128)}) custom-call(f32[4,64,512]{2,1,0:T(8,128)} %tile_hbm.1, f32[256,256]{1,0:T(8,128)} %epoch_hbm.1, s32[1,64]{1,0:T(1,128)} %bitcast.2, f32[1,64]{1,0:T(1,128)} %bitcast.3, f32[64,256]{1,0:T(8,128)} %curves_hbm.1), custom_call_target="tpu_custom_call" | custom-call | tf_op jit(solution)/shard_map/cg/pallas_call | solution.py:269
  37.6 0.0 copy-start
  37.7 1.5 %copy.9 = f32[64,256]{1,0:T(8,128)} copy(f32[64,256]{1,0:T(8,128)} %get-tuple-element.4) | data formatting | bytes 131072
  39.2 0.0 copy-done
  39.2 0.6 %copy.10 = f32[64,256]{1,0:T(8,128)} copy(f32[64,256]{1,0:T(8,128)S(1)} %copy-done) | data formatting | bytes 131072
Async XLA Ops:
  37.6 1.5 %copy-start = (f32[64,256]{1,0:T(8,128)S(1)}, f32[64,256]{1,0:T(8,128)}, u32[]{:S(2)}) copy-start(f32[64,256]{1,0:T(8,128)} %get-tuple-element.5) | copy-start | bytes 196612

commit v3 on v2

--- a/solution.py
+++ b/solution.py
@@ -10,7 +10,7 @@
 
 MESH = pl.DeviceIdType.MESH
 HALVES = 2
-GROUP = 2
+GROUP = 4
 
 
 def flip(index, bits):
@@ -87,8 +87,8 @@
     def greet(target):
         pl.semaphore_signal(barrier, inc=1, device_id=target, device_id_type=MESH)
 
-    direct = [*range(GROUP, R, GROUP), *range(1, GROUP)]
-    for d in direct:
+    direct = [*range(GROUP, R, GROUP), 2, 1]
+    for d in direct + [3]:
         greet(row_target(d))
     for j in range(1, C):
         greet(col_target(j))
@@ -110,7 +110,7 @@
     def row_copy(op, h, d):
         near = d % GROUP
         far = d - near
-        held, step = (far, near) if far and near else (0, d)
+        held, step = (far, near) if far and near else (2, 1) if d == 3 else (0, d)
         block = gathered.at[op, h, flip(me_row, held)]
         return remote(block, block, row_send.at[op, h, d], row_recv.at[op, h, d], row_target(step))
 
@@ -141,13 +141,15 @@
         for h in range(HALVES):
             for far in range(GROUP, R, GROUP):
                 row_arrival(op, h, far).wait_recv()
-                for near in range(1, GROUP):
+                for near in (3, 1, 2):
                     row_copy(op, h, far + near).start()
+            row_arrival(op, h, 2).wait_recv()
+            row_copy(op, h, 3).start()
 
     def multiply(op):
         for h in range(HALVES):
             for d in range(1, R):
-                if d < GROUP or d % GROUP:
+                if d != 2 and d % GROUP:
                     row_arrival(op, h, d).wait_recv()
             block = split(gathered[op, h].reshape(R * rows, width))
             product = dot3((tile_high[...], tile_low[...]), block)
@@ -199,7 +201,7 @@
             jnp.sum(value[:, 128:], axis=1, keepdims=True),
         )
 
-    pl.semaphore_wait(barrier, len(direct) + C - 1)
+    pl.semaphore_wait(barrier, len(direct) + 1 + C - 1)
     spread(0, first)
     for load in loads[3:]:
         load.wait()
@@ -285,10 +287,13 @@
         ],
         compiler_params=pltpu.CompilerParams(
             collective_id=0, has_side_effects=True,
-
+            vmem_limit_bytes=min(2 * held + (8 << 20), 60 * 1024 * 1024),
         ),
         name="cg",
-    )(kernel_configs, epoch_kernel, lengths.reshape(1, -1), noise.reshape(1, -1), curves)
+    )(*[
+        pltpu.with_memory_space_constraint(value, pltpu.HBM)
+        for value in (kernel_configs, epoch_kernel, lengths.reshape(1, -1), noise.reshape(1, -1), curves)
+    ])
 
 
 def solution(mesh):

time: 40 us -> 35.3 us (0.88)
  Pallas kernels: 37 us -> 33.2 us
  local copies, waits for them, and re-layouts: 2.14 us -> 1.26 us
    pallas_call x1, Pallas kernels: 37 us -> 33.2 us  [per_device(): pl.pallas_call(functools.partial(kernel, R, C), out_shape=[jax.ShapeDtype...]
    unnamed x4 -> x2, local copies, waits for them, and re-layouts: 2.14 us -> 1.26 us
where the time goes in v3:
time: 35.3 us; the launch traced here: 35.1 us
  Pallas kernels  33.2 us (94%)
  local copies, waits for them, and re-layouts  1.26 us (4%)
  between operations  0.64 us (2%)
    pallas_call x1, Pallas kernels, per_device(): pl.pallas_call(functools.partial(kernel, R, C), out_shape=[jax.ShapeDtype...  33.2 us
    unnamed x2, local copies, waits for them, and re-layouts  1.26 us

profile of v3, /device:TPU:0, one launch (start us, length us, event | category | flops | bytes accessed | tf_op | source)
XLA Modules:
  0.0 35.1 jit_solution(4528751077210095754)
XLA Ops:
  0.6 33.2 %cg.1 = (f32[64,256]{1,0:T(8,128)S(1)}, f32[64,256]{1,0:T(8,128)S(1)}) custom-call(f32[4,64,512]{2,1,0:T(8,128)} %tile_hbm.1, f32[256,256]{1,0:T(8,128)} %epoch_hbm.1, s32[1,64]{1,0:T(1,128)} %bitcast.2, f32[1,64]{1,0:T(1,128)} %bitcast.3, f32[64,256]{1,0:T(8,128)} %curves_hbm.1), custom_call_target="tpu_custom_call" | custom-call | tf_op jit(solution)/shard_map/cg/pallas_call | solution.py:271
  33.9 0.6 %copy.9 = f32[64,256]{1,0:T(8,128)} copy(f32[64,256]{1,0:T(8,128)S(1)} %get-tuple-element.4) | data formatting | bytes 131072
  34.5 0.6 %copy.10 = f32[64,256]{1,0:T(8,128)} copy(f32[64,256]{1,0:T(8,128)S(1)} %get-tuple-element.5) | data formatting | bytes 131072
